TPU v7x, 512 devices: a whole 4x4x16 slice. The times are simulated.
512 devices in a mesh: seq: 8 (over x, core), tok: 64 (over z, y).
Axes of the slice: x: 4, y: 4, z: 16, core: 2. Of those that a mesh axis runs over, the one named last changes fastest.
Arguments:
- block_in: bfloat16 [8, 256, 1024], P('seq'), may hold values from -6 to 6
- accept: int32 [2, 8, 256], P(None, 'seq'), may hold values 0 or 1
- cache_len: int32 [8], P('seq'), may hold values from 8192 to 16384, as said below
- slot_page: int32 [8, 192], P('seq', 'tok'), may hold values from -1 to 127, as said below
- cache_kv: bfloat16 [8, 192, 128, 2048], P('seq', 'tok'), as said below
- w_query: bfloat16 [1024, 1024], P('seq', 'tok'), may hold values from -0.25 to 0.25
- w_key_value: bfloat16 [1024, 2048], P('seq', 'tok'), may hold values from -0.375 to 0.375
- w_out: bfloat16 [1024, 1024], P('seq', 'tok'), may hold values from -0.1875 to 0.1875
- gain_attn: float32 [1024], replicated, may hold values from 0.1 to 1.9
- w_up: bfloat16 [1024, 4096], P('seq', 'tok'), may hold values from -0.1875 to 0.1875
- w_down: bfloat16 [4096, 1024], P('tok', 'seq'), may hold values from -0.09375 to 0.09375
- gain_mlp: float32 [1024], replicated, may hold values from 0.1 to 1.9
Outputs:
- refined: bfloat16 [8, 256, 1024], P('seq')
Inputs may be any that keep to these rules, and one draw needn't show every extreme that they name: `cache_len`: one sequence has exactly 16384 cached tokens. `slot_page`: slots j * 3 to (j + 1) * 3 - 1 of a row are those of index j of tok. Each page 0 to ceil(cache_len[s] / 128) - 1 of sequence s is in exactly one slot of row s, every other slot holds -1, and in every row some index of tok has all 3 of its slots filled. `cache_kv`: finite values; entries of empty slots are arbitrary.
All inputs are finite; a program needn't handle non-finite values. No bound on the sum of `accept` on one device may be relied on, other than what follows from the above.
Results may differ from a plain program's by a relative error of at most 0.035.
The roundings to bfloat16 on the way count: a program that leaves them out, or rounds other values in their place, can miss the bound.
Values may be sent and summed in bfloat16 or wider, within the bound.
A program may use at most 64 MiB of HBM per device.

v0:
```python
import jax
import jax.numpy as jnp
from jax import lax
from jax.sharding import PartitionSpec as P

HEADS = 16
HEAD_DIM = 64
EPSILON = 1e-05
FLOOR_SCORE = -1e30


def layer_norm(values, gain_vec):
    average = jnp.mean(values, axis=-1, keepdims=True)
    centered = values - average
    variance = jnp.mean(centered * centered, axis=-1, keepdims=True)
    return centered * lax.rsqrt(variance + EPSILON) * gain_vec


def merge_state(earlier, later):
    overall = jnp.maximum(earlier[0], later[0])
    early_factor = jnp.exp(earlier[0] - overall)
    late_factor = jnp.exp(later[0] - overall)
    totals = earlier[1] * early_factor + later[1] * late_factor
    weighted = earlier[2] * early_factor[..., None] + later[2] * late_factor[..., None]
    return (overall, totals, weighted)


def page_partial(queries, page_keys, page_values, usable):
    scores = jnp.einsum(
        "sqhe,skhe->sqhk", queries, page_keys, preferred_element_type=jnp.float32
    ) * HEAD_DIM ** (-0.5)
    masked = jnp.where(usable[:, None, None, :], scores, FLOOR_SCORE)
    peaks = jnp.max(masked, axis=-1)
    weights = jnp.where(usable[:, None, None, :], jnp.exp(masked - peaks[..., None]), 0.0).astype(
        jnp.bfloat16
    )
    weighted = jnp.einsum(
        "sqhk,skhe->sqhe", weights, page_values, preferred_element_type=jnp.float32
    )
    totals = jnp.sum(weights.astype(jnp.float32), axis=-1)
    return (peaks, totals, weighted)


def shards(
    block_in,
    accept,
    cache_len,
    slot_page,
    cache_kv,
    w_query,
    w_key_value,
    w_out,
    gain_attn,
    w_up,
    w_down,
    gain_mlp,
):
    groups, block_len, model_width = block_in.shape
    tok_parts = lax.axis_size("tok")
    tok_dev = block_len // tok_parts
    slot_count = cache_kv.shape[1]
    page_len = cache_kv.shape[2]
    own_index = lax.axis_index("tok")
    rows_q, rows_kv, rows_o, rows_up, cols_down = (
        lax.all_gather(w_query, "seq", axis=0, tiled=True),
        lax.all_gather(w_key_value, "seq", axis=0, tiled=True),
        lax.all_gather(w_out, "seq", axis=0, tiled=True),
        lax.all_gather(w_up, "seq", axis=0, tiled=True),
        lax.all_gather(w_down, "seq", axis=1, tiled=True),
    )
    full_q, full_kv, full_o = (
        lax.all_gather(rows_q, "tok", axis=1, tiled=True),
        lax.all_gather(rows_kv, "tok", axis=1, tiled=True),
        lax.all_gather(rows_o, "tok", axis=1, tiled=True),
    )

    def attend(inputs):
        flat_all = inputs.reshape(groups * block_len, model_width)
        own_rows = lax.dynamic_slice_in_dim(inputs, own_index * tok_dev, tok_dev, 1)
        flat_rows = own_rows.reshape(groups * tok_dev, model_width)
        queries = jnp.dot(flat_all, full_q, preferred_element_type=jnp.float32).astype(jnp.bfloat16)
        own_pair = jnp.dot(flat_rows, full_kv, preferred_element_type=jnp.float32).astype(
            jnp.bfloat16
        )
        own_pair = own_pair.reshape(groups, tok_dev, 2 * model_width)
        queries = queries.reshape(groups, block_len, HEADS, HEAD_DIM)
        own_keys = own_pair[..., :model_width].reshape(groups, tok_dev, HEADS, HEAD_DIM)
        own_values = own_pair[..., model_width:].reshape(groups, tok_dev, HEADS, HEAD_DIM)
        carry_state = page_partial(
            queries, own_keys, own_values, jnp.ones((groups, tok_dev), dtype=bool)
        )

        def slot_step(slot_index, carry_state):
            page_pair = lax.dynamic_index_in_dim(cache_kv, slot_index, 1, keepdims=False)
            page_no = lax.dynamic_index_in_dim(slot_page, slot_index, 1, keepdims=False)
            positions = page_no[:, None] * page_len + jnp.arange(page_len, dtype=jnp.int32)[None, :]
            usable = (page_no[:, None] >= 0) & (positions < cache_len[:, None])
            page_keys = page_pair[..., :model_width].reshape(groups, page_len, HEADS, HEAD_DIM)
            page_values = page_pair[..., model_width:].reshape(groups, page_len, HEADS, HEAD_DIM)
            return merge_state(carry_state, page_partial(queries, page_keys, page_values, usable))

        peaks, totals, weighted = lax.fori_loop(0, slot_count, slot_step, carry_state)
        peak_parts = lax.all_to_all(peaks[None], "tok", split_axis=2, concat_axis=0, tiled=True)
        total_parts = lax.all_to_all(totals[None], "tok", split_axis=2, concat_axis=0, tiled=True)
        weighted_parts = lax.all_to_all(
            weighted.reshape(groups, block_len, model_width)[None],
            "tok",
            split_axis=2,
            concat_axis=0,
            tiled=True,
        )
        overall = jnp.max(peak_parts, axis=0)
        factor = jnp.exp(peak_parts - overall[None])
        denominator = jnp.sum(total_parts * factor, axis=0)
        split_parts = weighted_parts.reshape(weighted_parts.shape[:-1] + (HEADS, HEAD_DIM))
        numerator = jnp.sum(split_parts * factor[..., None], axis=0)
        attention = (numerator / denominator[..., None]).reshape(
            numerator.shape[:-2] + (model_width,)
        )
        attention = attention.astype(jnp.bfloat16).reshape(groups * tok_dev, model_width)
        residual = flat_rows.astype(jnp.float32) + jnp.dot(
            attention, full_o, preferred_element_type=jnp.float32
        )
        return (
            layer_norm(residual, gain_attn)
            .astype(jnp.bfloat16)
            .reshape(groups, tok_dev, model_width)
        )

    def feed(settled):
        products = jnp.einsum(
            "gtd,df->gtf",
            lax.all_gather(settled, "tok", axis=1, tiled=True),
            rows_up,
            preferred_element_type=jnp.float32,
        )
        hidden = jax.nn.gelu(products, approximate=False).astype(jnp.bfloat16)
        mlp_term = jnp.einsum("gtf,fd->gtd", hidden, cols_down, preferred_element_type=jnp.float32)
        projected = lax.psum_scatter(mlp_term, "tok", scatter_dimension=1, tiled=True)
        finished = layer_norm(settled.astype(jnp.float32) + projected, gain_mlp).astype(
            jnp.bfloat16
        )
        return lax.all_gather(finished, "tok", axis=1, tiled=True)

    first_out = feed(attend(block_in))
    second_in = jnp.where(accept[0][..., None] == 1, first_out, block_in)
    second_out = feed(attend(second_in))
    return jnp.where(accept[1][..., None] == 1, second_out, second_in)


def solution(mesh):
    in_specs = (
        P("seq", None, None),
        P(None, "seq", None),
        P("seq"),
        P("seq", "tok"),
        P("seq", "tok", None, None),
        P("seq", "tok"),
        P("seq", "tok"),
        P("seq", "tok"),
        P(),
        P("seq", "tok"),
        P("tok", "seq"),
        P(),
    )
    out_specs = P("seq", None, None)
    return jax.shard_map(shards, mesh=mesh, in_specs=in_specs, out_specs=out_specs, check_vma=False)
```

profile of v0, /device:TPU:2, one launch (start us, length us, event | category | flops | bytes accessed | tf_op | source)
XLA Modules:
  0.0 1601.0 jit_solution(3491275169055620532)
XLA Ops:
  6.5 16.2 %all_gather.38 = bf16[1024,16]{0,1:T(8,128)(2,1)} all-gather(bf16[128,16]{0,1:T(8,128)(2,1)} %param.21), channel_id=1, replica_groups=mesh['seq'=8,'tok'=64] {'seq'}, dimensions={0}, use_global_device_ids=true | all-gather | bytes 36864 | tf_op jit(solution)/shard_map/all_gather | solution.py:65
  22.9 13.1 all_gather.36
  38.0 126.6 %all-gather.10.cloned.1.call-done = bf16[1024,1024]{0,1:T(8,128)(2,1)} async-done(((bf16[1024,16]{0,1:T(8,128)(2,1)}), bf16[1024,1024]{0,1:T(8,128)(2,1)}) %all-gather.10.cloned.1.call-update) | async-done | bytes 2097168 | tf_op jit(solution)/shard_map/all_gather | solution.py:72
  167.1 143.0 %all-gather.8.cloned.1.call-done = bf16[1024,2048]{0,1:T(8,128)(2,1)} async-done(((bf16[1024,32]{0,1:T(8,128)(2,1)}), bf16[1024,2048]{0,1:T(8,128)(2,1)}) %all-gather.8.cloned.1.call-update) | async-done | bytes 4194320 | tf_op jit(solution)/shard_map/all_gather | solution.py:73
  314.3 14.3 while.34
  329.3 8.9 all-to-all-start.1
  339.0 15.4 all-to-all-done.1
  361.0 14.3 all-to-all-done.2
  380.9 12.7 all_gather.40
  393.6 11.0 all_gather.43
  404.6 11.2 all_gather.44
  428.6 106.4 %all-gather.12.cloned.1.call-done = bf16[1024,1024]{0,1:T(8,128)(2,1)} async-done(((bf16[1024,16]{0,1:T(8,128)(2,1)}), bf16[1024,1024]{0,1:T(8,128)(2,1)}) %all-gather.12.cloned.1.call-update) | async-done | bytes 2097168 | tf_op jit(solution)/shard_map/all_gather | solution.py:74
  537.6 98.1 %all-gather.2 = bf16[64,4,1024]{2,1,0:T(4,128)(2,1)S(1)} all-gather(bf16[1,4,1024]{2,1,0:T(4,128)(2,1)S(1)} %fusion.126), channel_id=2, replica_groups=mesh['seq'=8,'tok'=64] {'tok'}, dimensions={0}, use_global_device_ids=true | all-gather | bytes 532480 | tf_op jit(solution)/shard_map/all_gather | solution.py:133
  641.7 266.9 %all-reduce.5.cloned.1.call-done = f32[1,256,1024]{2,1,0:T(8,128)} async-done(((f32[1,256,1024]{2,1,0:T(8,128)}), f32[1,256,1024]{2,1,0:T(8,128)}) %all-reduce.5.cloned.1.call-update) | async-done | bytes 1048592
  911.5 98.7 %all_gather.45 = bf16[1,256,1024]{2,0,1:T(2,128)(2,1)S(1)} all-gather(bf16[1,4,1024]{2,0,1:T(2,128)(2,1)S(1)} %copy.77), channel_id=1, replica_groups=mesh['seq'=8,'tok'=64] {'tok'}, dimensions={1}, use_global_device_ids=true | all-gather | bytes 532480 | tf_op jit(solution)/shard_map/all_gather | solution.py:143
  1015.7 14.5 while.35
  1030.9 10.5 all-to-all-start.4
  1042.2 15.4 all-to-all-done.4
  1057.6 5.9 all-to-all-start.5
  1065.5 16.6 %all-to-all-done.5 = f32[1,1,256,16]{3,1,0,2:T(1,128)S(1)} async-done(((f32[1,1,256,16]{3,1,0,2:T(1,128)}), f32[1,1,256,16]{3,1,0,2:T(1,128)S(1)}, u32[]{:S(2)}, u32[]{:S(2)}) %all-to-all-start.5) | async-done | bytes 16416 | tf_op jit(solution)/shard_map/all_to_all | solution.py:104
  1092.5 28.2 %all-to-all-done.3 = f32[1,1,256,1024]{3,1,0,2:T(1,128)S(1)} async-done(((f32[1,1,256,1024]{3,1,0,2:T(1,128)}), f32[1,1,256,1024]{3,1,0,2:T(1,128)S(1)}, u32[]{:S(2)}, u32[]{:S(2)}) %all-to-all-start.3) | async-done | bytes 1048608 | tf_op jit(solution)/shard_map/all_to_all | solution.py:105
  1125.4 99.8 %all-gather.3 = bf16[64,4,1024]{2,1,0:T(4,128)(2,1)S(1)} all-gather(bf16[1,4,1024]{2,1,0:T(4,128)(2,1)S(1)} %fusion.127), channel_id=3, replica_groups=mesh['seq'=8,'tok'=64] {'tok'}, dimensions={0}, use_global_device_ids=true | all-gather | bytes 532480 | tf_op jit(solution)/shard_map/all_gather | solution.py:133
  1227.3 265.2 %all-reduce.7.cloned.1.call-done = f32[1,256,1024]{2,1,0:T(8,128)} async-done(((f32[1,256,1024]{2,1,0:T(8,128)}), f32[1,256,1024]{2,1,0:T(8,128)}) %all-reduce.7.cloned.1.call-update) | async-done | bytes 1048592
  1495.3 98.1 %all_gather.47 = bf16[1,256,1024]{2,0,1:T(2,128)(2,1)S(1)} all-gather(bf16[1,4,1024]{2,0,1:T(2,128)(2,1)S(1)} %copy.87), channel_id=1, replica_groups=mesh['seq'=8,'tok'=64] {'tok'}, dimensions={1}, use_global_device_ids=true | all-gather | bytes 532480 | tf_op jit(solution)/shard_map/all_gather | solution.py:143
  (171 shorter events, 100.5 us)
Async XLA Ops:
  6.5 158.0 %copy-start.2 = (bf16[1,256,1024]{2,1,0:T(8,128)(2,1)S(1)}, bf16[1,256,1024]{2,1,0:T(8,128)(2,1)}, u32[]{:S(2)}) copy-start(bf16[1,256,1024]{2,1,0:T(8,128)(2,1)} %param.16) | copy-start | bytes 1572868
  6.5 158.0 %all-gather.10.cloned.1.call-start = ((), (), s32[]{:S(2)}) async-start(), calls=%async_computation.7 | async-start | bytes 2129920 | tf_op jit(solution)/shard_map/all_gather | solution.py:72
  22.8 287.3 %all-gather.8.cloned.1.call-start = ((), (), s32[]{:S(2)}) async-start(), calls=%async_computation.6 | async-start | bytes 4259840 | tf_op jit(solution)/shard_map/all_gather | solution.py:73
  167.1 147.2 %copy-start.5 = (s32[1,3]{1,0:T(1,128)S(1)}, s32[1,3]{1,0:T(1,128)}, u32[]{:S(2)}) copy-start(s32[1,3]{1,0:T(1,128)} %param.19) | copy-start | bytes 40
  329.3 25.0 %all-to-all-start.1 = ((f32[1,1,256,16]{3,1,0,2:T(1,128)}), f32[1,1,256,16]{3,1,0,2:T(1,128)S(1)}, u32[]{:S(2)}, u32[]{:S(2)}) async-start(f32[1,1,256,16]{3,1,0,2:T(1,128)} %bitcast.47), calls=%async_computation.1 | async-start | bytes 262144 | tf_op jit(solution)/shard_map/all_to_all | solution.py:103
  354.4 20.9 %all-to-all-start.2 = ((f32[1,1,256,16]{3,1,0,2:T(1,128)}), f32[1,1,256,16]{3,1,0,2:T(1,128)S(1)}, u32[]{:S(2)}, u32[]{:S(2)}) async-start(f32[1,1,256,16]{3,1,0,2:T(1,128)} %bitcast.49), calls=%async_computation.2 | async-start | bytes 262144 | tf_op jit(solution)/shard_map/all_to_all | solution.py:104
  359.0 21.9 %copy-start.9 = (bf16[128,16]{0,1:T(8,128)(2,1)S(1)}, bf16[128,16]{0,1:T(8,128)(2,1)}, u32[]{:S(2)}) copy-start(bf16[128,16]{0,1:T(8,128)(2,1)} %param.23) | copy-start | bytes 12292
  359.0 34.6 %copy-start.6 = (bf16[128,64]{0,1:T(8,128)(2,1)S(1)}, bf16[128,64]{0,1:T(8,128)(2,1)}, u32[]{:S(2)}) copy-start(bf16[128,64]{0,1:T(8,128)(2,1)} %param.25) | copy-start | bytes 49156
  359.0 45.6 %copy-start.7 = (bf16[64,128]{1,0:T(8,128)(2,1)S(1)}, bf16[64,128]{1,0:T(8,128)(2,1)}, u32[]{:S(2)}) copy-start(bf16[64,128]{1,0:T(8,128)(2,1)} %param.26) | copy-start | bytes 49156
  375.3 50.2 %all-to-all-start = ((f32[1,1,256,1024]{3,1,0,2:T(1,128)}), f32[1,1,256,1024]{3,1,0,2:T(1,128)}, u32[]{:S(2)}, u32[]{:S(2)}) async-start(f32[1,1,256,1024]{3,1,0,2:T(1,128)} %copy.74), calls=%async_computation | async-start | bytes 2097152 | tf_op jit(solution)/shard_map/all_to_all | solution.py:105
  380.8 154.2 %all-gather.12.cloned.1.call-start = ((), (), s32[]{:S(2)}) async-start(), calls=%async_computation.8 | async-start | bytes 2129920 | tf_op jit(solution)/shard_map/all_gather | solution.py:74
  393.5 515.0 %all-reduce.5.cloned.1.call-start = ((), (), s32[]{:S(2)}) async-start(), calls=%async_computation.9 | async-start | bytes 2097152
  418.2 116.8 %copy-start.3 = (bf16[1,256,1024]{2,1,0:T(8,128)(2,1)S(1)}, bf16[1,256,1024]{2,1,0:T(8,128)(2,1)}, u32[]{:S(2)}) copy-start(bf16[1,256,1024]{2,1,0:T(8,128)(2,1)} %param.16) | copy-start | bytes 1572868
  425.5 112.1 %copy-start.4 = (f32[1024]{0:T(1024)S(1)}, f32[1024]{0:T(1024)}, u32[]{:S(2)}) copy-start(f32[1024]{0:T(1024)} %param.24) | copy-start | bytes 12292
  635.8 5.9 copy-start.10
  635.8 274.8 %copy-start.8 = (f32[1024]{0:T(1024)S(1)}, f32[1024]{0:T(1024)}, u32[]{:S(2)}) copy-start(f32[1024]{0:T(1024)} %param.27) | copy-start | bytes 12292
  908.5 101.9 %copy-start.11 = (bf16[1024,1024]{0,1:T(8,128)(2,1)S(1)}, bf16[1024,1024]{0,1:T(8,128)(2,1)}, u32[]{:S(2)}) copy-start(bf16[1024,1024]{0,1:T(8,128)(2,1)} %all-gather.10.cloned.1.call-done) | copy-start | bytes 6291460
  1010.4 1.0 copy-start
  1030.9 26.7 %all-to-all-start.4 = ((f32[1,1,256,16]{3,1,0,2:T(1,128)}), f32[1,1,256,16]{3,1,0,2:T(1,128)S(1)}, u32[]{:S(2)}, u32[]{:S(2)}) async-start(f32[1,1,256,16]{3,1,0,2:T(1,128)} %bitcast.70), calls=%async_computation.4 | async-start | bytes 262144 | tf_op jit(solution)/shard_map/all_to_all | solution.py:103
  1057.6 24.5 %all-to-all-start.5 = ((f32[1,1,256,16]{3,1,0,2:T(1,128)}), f32[1,1,256,16]{3,1,0,2:T(1,128)S(1)}, u32[]{:S(2)}, u32[]{:S(2)}) async-start(f32[1,1,256,16]{3,1,0,2:T(1,128)} %bitcast.72), calls=%async_computation.5 | async-start | bytes 262144 | tf_op jit(solution)/shard_map/all_to_all | solution.py:104
  1082.1 38.6 %all-to-all-start.3 = ((f32[1,1,256,1024]{3,1,0,2:T(1,128)}), f32[1,1,256,1024]{3,1,0,2:T(1,128)S(1)}, u32[]{:S(2)}, u32[]{:S(2)}) async-start(f32[1,1,256,1024]{3,1,0,2:T(1,128)} %copy.84), calls=%async_computation.3 | async-start | bytes 2097152 | tf_op jit(solution)/shard_map/all_to_all | solution.py:105
  1087.1 405.4 %all-reduce.7.cloned.1.call-start = ((), (), s32[]{:S(2)}) async-start(), calls=%async_computation.10 | async-start | bytes 2097152
  1089.8 33.0 %copy-start.1 = (bf16[1,256,1024]{2,1,0:T(8,128)(2,1)S(1)}, bf16[1,256,1024]{2,1,0:T(8,128)(2,1)}, u32[]{:S(2)}) copy-start(bf16[1,256,1024]{2,1,0:T(8,128)(2,1)} %copy-done) | copy-start | bytes 1572868
Sparse Core Ops, SparseCore 0:
  22.9 141.5 all-gather.9
  167.5 142.5 all-gather.7
  393.7 141.2 all-gather.11
  639.8 268.6 all-reduce.4
  1227.5 265.0 all-reduce.6
where the time goes:
time: 1600 us
  waiting for transfers between devices  1000 us (62%)
  blocking collectives  459 us (29%)
  starting transfers between devices  40.8 us (3%)
  matrix products  29.6 us (2%)
  other arithmetic  28.5 us (2%)
  local copies, waits for them, and re-layouts  22.3 us (1%)
    unnamed x7, waiting for transfers between devices  532 us
    all_gather x2, blocking collectives, feed(): lax.all_gather(settled, 'tok', axis=1, tiled=True)  198 us
    all_gather x2, blocking collectives, feed(): return lax.all_gather(finished, 'tok', axis=1, tiled=True)  197 us
    all_gather x1, waiting for transfers between devices, shards(): lax.all_gather(rows_kv, 'tok', axis=1, tiled=True)  143 us
    all_gather x1, waiting for transfers between devices, shards(): lax.all_gather(rows_q, 'tok', axis=1, tiled=True)  127 us
    all_gather x1, waiting for transfers between devices, shards(): lax.all_gather(rows_o, 'tok', axis=1, tiled=True)  106 us
    all_to_all x2, waiting for transfers between devices, attend(): lax.all_to_all(weighted.reshape(groups, block_len, model_width)[None], 't...  32.7 us
  transfers between devices with their start and end apart: 11, of which 11 were waited for; matrix products, arithmetic and copies ran while one was open for 2% of the time, Pallas kernels for 0%

commit v1 on v0

--- a/solution.py
+++ b/solution.py
@@ -130,7 +130,9 @@
     def feed(settled):
         products = jnp.einsum(
             "gtd,df->gtf",
-            lax.all_gather(settled, "tok", axis=1, tiled=True),
+            jnp.concatenate(
+                lax.all_to_all(jnp.stack([settled] * lax.axis_size("tok")), "tok", 0, 0), axis=1
+            ),
             rows_up,
             preferred_element_type=jnp.float32,
         )

time: 1600 us -> 1490 us (0.931)
  blocking collectives: 459 us -> 290 us
  waiting for transfers between devices: 1000 us -> 1040 us
    all_gather x2 -> x0, blocking collectives: 198 us -> none  [feed(): lax.all_gather(settled, 'tok', axis=1, tiled=True)]
    all_to_all x2, waiting for transfers between devices: 32.7 us -> 66.5 us  [attend(): lax.all_to_all(weighted.reshape(groups, block_len, model_width)[None], 't...]
    all_to_all x0 -> x1, blocking collectives: none -> 28.6 us  [feed(): lax.all_to_all(jnp.stack([settled] * lax.axis_size('tok')), 'tok', 0, 0)]
  transfers between devices with their start and end apart: 11 -> 12, of which waited for: 11 -> 12; matrix products, arithmetic and copies ran while one was open for 2% -> 2% of each run, Pallas kernels for 0% -> 0%
where the time goes in v1:
time: 1490 us; the launch traced here: 1480 us
  waiting for transfers between devices  1040 us (70%)
  blocking collectives  290 us (19%)
  starting transfers between devices  50.9 us (3%)
  other arithmetic  29.6 us (2%)
  matrix products  28.7 us (2%)
  local copies, waits for them, and re-layouts  23.4 us (2%)
    unnamed x7, waiting for transfers between devices  537 us
    all_gather x2, blocking collectives, feed(): return lax.all_gather(finished, 'tok', axis=1, tiled=True)  197 us
    all_gather x1, waiting for transfers between devices, shards(): lax.all_gather(rows_kv, 'tok', axis=1, tiled=True)  143 us
    all_gather x1, waiting for transfers between devices, shards(): lax.all_gather(rows_q, 'tok', axis=1, tiled=True)  127 us
    all_gather x1, waiting for transfers between devices, shards(): lax.all_gather(rows_o, 'tok', axis=1, tiled=True)  106 us
    all_to_all x2, waiting for transfers between devices, attend(): lax.all_to_all(weighted.reshape(groups, block_len, model_width)[None], 't...  66.5 us
    all_to_all x2, waiting for transfers between devices, attend(): lax.all_to_all(totals[None], 'tok', split_axis=2, concat_axis=0, tiled=True)  31.6 us
    all_to_all x2, waiting for transfers between devices, attend(): lax.all_to_all(peaks[None], 'tok', split_axis=2, concat_axis=0, tiled=True)  30.8 us
  transfers between devices with their start and end apart: 12, of which 12 were waited for; matrix products, arithmetic and copies ran while one was open for 2% of the time, Pallas kernels for 0%

profile of v1, /device:TPU:2, one launch (start us, length us, event | category | flops | bytes accessed | tf_op | source)
XLA Modules:
  0.0 1483.4 jit_solution(6126258030013228949)
XLA Ops:
  6.5 16.2 %all_gather.32 = bf16[1024,16]{0,1:T(8,128)(2,1)} all-gather(bf16[128,16]{0,1:T(8,128)(2,1)} %param.21), channel_id=1, replica_groups=mesh['seq'=8,'tok'=64] {'seq'}, dimensions={0}, use_global_device_ids=true | all-gather | bytes 36864 | tf_op jit(solution)/shard_map/all_gather | solution.py:65
  22.9 13.1 all_gather.30
  38.0 126.6 %all-gather.6.cloned.1.call-done = bf16[1024,1024]{0,1:T(8,128)(2,1)} async-done(((bf16[1024,16]{0,1:T(8,128)(2,1)}), bf16[1024,1024]{0,1:T(8,128)(2,1)}) %all-gather.6.cloned.1.call-update) | async-done | bytes 2097168 | tf_op jit(solution)/shard_map/all_gather | solution.py:72
  167.1 143.0 %all-gather.4.cloned.1.call-done = bf16[1024,2048]{0,1:T(8,128)(2,1)} async-done(((bf16[1024,32]{0,1:T(8,128)(2,1)}), bf16[1024,2048]{0,1:T(8,128)(2,1)}) %all-gather.4.cloned.1.call-update) | async-done | bytes 4194320 | tf_op jit(solution)/shard_map/all_gather | solution.py:73
  314.3 14.3 while.34
  329.3 8.9 all-to-all-start.1
  339.0 15.4 %all-to-all-done.1 = f32[1,1,256,16]{3,1,0,2:T(1,128)S(1)} async-done(((f32[1,1,256,16]{3,1,0,2:T(1,128)}), f32[1,1,256,16]{3,1,0,2:T(1,128)S(1)}, u32[]{:S(2)}, u32[]{:S(2)}) %all-to-all-start.1) | async-done | bytes 16416 | tf_op jit(solution)/shard_map/all_to_all | solution.py:103
  360.9 14.3 all-to-all-done.2
  380.9 12.8 all_gather.34
  398.9 26.6 %all-to-all-done = f32[1,1,256,1024]{3,1,0,2:T(1,128)} async-done(((f32[1,1,256,1024]{3,1,0,2:T(1,128)}), f32[1,1,256,1024]{3,1,0,2:T(1,128)}, u32[]{:S(2)}, u32[]{:S(2)}) %all-to-all-start) | async-done | bytes 1048608 | tf_op jit(solution)/shard_map/all_to_all | solution.py:105
  428.6 106.5 %all-gather.8.cloned.1.call-done = bf16[1024,1024]{0,1:T(8,128)(2,1)} async-done(((bf16[1024,16]{0,1:T(8,128)(2,1)}), bf16[1024,1024]{0,1:T(8,128)(2,1)}) %all-gather.8.cloned.1.call-update) | async-done | bytes 2097168 | tf_op jit(solution)/shard_map/all_gather | solution.py:74
  538.7 10.3 all-to-all-start.3
  549.0 11.6 all_gather.36
  560.6 11.0 all_gather.37
  578.2 271.7 %all-reduce.5.cloned.1.call-done = f32[1,256,1024]{2,1,0:T(8,128)} async-done(((f32[1,256,1024]{2,1,0:T(8,128)}), f32[1,256,1024]{2,1,0:T(8,128)}) %all-reduce.5.cloned.1.call-update) | async-done | bytes 1048592
  852.9 98.7 %all_gather.38 = bf16[1,256,1024]{2,0,1:T(2,128)(2,1)S(1)} all-gather(bf16[1,4,1024]{2,0,1:T(2,128)(2,1)S(1)} %copy.77), channel_id=1, replica_groups=mesh['seq'=8,'tok'=64] {'tok'}, dimensions={1}, use_global_device_ids=true | all-gather | bytes 532480 | tf_op jit(solution)/shard_map/all_gather | solution.py:145
  957.0 14.5 while.35
  972.3 10.6 all-to-all-start.5
  983.7 15.4 %all-to-all-done.5 = f32[1,1,256,16]{3,1,0,2:T(1,128)S(1)} async-done(((f32[1,1,256,16]{3,1,0,2:T(1,128)}), f32[1,1,256,16]{3,1,0,2:T(1,128)S(1)}, u32[]{:S(2)}, u32[]{:S(2)}) %all-to-all-start.5) | async-done | bytes 16416 | tf_op jit(solution)/shard_map/all_to_all | solution.py:103
  1005.7 17.2 %all-to-all-done.6 = f32[1,1,256,16]{3,1,0,2:T(1,128)S(1)} async-done(((f32[1,1,256,16]{3,1,0,2:T(1,128)}), f32[1,1,256,16]{3,1,0,2:T(1,128)S(1)}, u32[]{:S(2)}, u32[]{:S(2)}) %all-to-all-start.6) | async-done | bytes 16416 | tf_op jit(solution)/shard_map/all_to_all | solution.py:104
  1034.4 39.8 %all-to-all-done.4 = f32[1,1,256,1024]{3,1,0,2:T(1,128)} async-done(((f32[1,1,256,1024]{3,1,0,2:T(1,128)}), f32[1,1,256,1024]{3,1,0,2:T(1,128)}, u32[]{:S(2)}, u32[]{:S(2)}) %all-to-all-start.4) | async-done | bytes 1048608 | tf_op jit(solution)/shard_map/all_to_all | solution.py:105
  1079.2 28.6 %all_to_all.88 = bf16[64,1,4,1024]{3,2,1,0:T(4,128)(2,1)S(1)} all-to-all(bf16[64,1,4,1024]{3,2,1,0:T(4,128)(2,1)S(1)} %stack.7), channel_id=1, replica_groups=mesh['seq'=8,'tok'=64] {'tok'}, dimensions={0} | all-to-all | bytes 1048576 | tf_op jit(solution)/shard_map/all_to_all | solution.py:134
  1110.1 265.0 %all-reduce.7.cloned.1.call-done = f32[1,256,1024]{2,1,0:T(8,128)} async-done(((f32[1,256,1024]{2,1,0:T(8,128)}), f32[1,256,1024]{2,1,0:T(8,128)}) %all-reduce.7.cloned.1.call-update) | async-done | bytes 1048592
  1377.8 98.1 %all_gather.39 = bf16[1,256,1024]{2,0,1:T(2,128)(2,1)S(1)} all-gather(bf16[1,4,1024]{2,0,1:T(2,128)(2,1)S(1)} %copy.87), channel_id=1, replica_groups=mesh['seq'=8,'tok'=64] {'tok'}, dimensions={1}, use_global_device_ids=true | all-gather | bytes 532480 | tf_op jit(solution)/shard_map/all_gather | solution.py:145
  (176 shorter events, 103.6 us)
Async XLA Ops:
  6.5 158.0 %copy-start.3 = (bf16[1,256,1024]{2,1,0:T(8,128)(2,1)S(1)}, bf16[1,256,1024]{2,1,0:T(8,128)(2,1)}, u32[]{:S(2)}) copy-start(bf16[1,256,1024]{2,1,0:T(8,128)(2,1)} %param.16) | copy-start | bytes 1572868
  6.5 158.0 %all-gather.6.cloned.1.call-start = ((), (), s32[]{:S(2)}) async-start(), calls=%async_computation.9 | async-start | bytes 2129920 | tf_op jit(solution)/shard_map/all_gather | solution.py:72
  22.8 287.3 %all-gather.4.cloned.1.call-start = ((), (), s32[]{:S(2)}) async-start(), calls=%async_computation.8 | async-start | bytes 4259840 | tf_op jit(solution)/shard_map/all_gather | solution.py:73
  167.1 147.2 %copy-start.6 = (s32[1,3]{1,0:T(1,128)S(1)}, s32[1,3]{1,0:T(1,128)}, u32[]{:S(2)}) copy-start(s32[1,3]{1,0:T(1,128)} %param.19) | copy-start | bytes 40
  329.3 25.0 %all-to-all-start.1 = ((f32[1,1,256,16]{3,1,0,2:T(1,128)}), f32[1,1,256,16]{3,1,0,2:T(1,128)S(1)}, u32[]{:S(2)}, u32[]{:S(2)}) async-start(f32[1,1,256,16]{3,1,0,2:T(1,128)} %bitcast.47), calls=%async_computation.1 | async-start | bytes 262144 | tf_op jit(solution)/shard_map/all_to_all | solution.py:103
  354.4 20.9 %all-to-all-start.2 = ((f32[1,1,256,16]{3,1,0,2:T(1,128)}), f32[1,1,256,16]{3,1,0,2:T(1,128)S(1)}, u32[]{:S(2)}, u32[]{:S(2)}) async-start(f32[1,1,256,16]{3,1,0,2:T(1,128)} %bitcast.49), calls=%async_computation.2 | async-start | bytes 262144 | tf_op jit(solution)/shard_map/all_to_all | solution.py:104
  359.0 21.9 %copy-start.10 = (bf16[128,16]{0,1:T(8,128)(2,1)S(1)}, bf16[128,16]{0,1:T(8,128)(2,1)}, u32[]{:S(2)}) copy-start(bf16[128,16]{0,1:T(8,128)(2,1)} %param.23) | copy-start | bytes 12292
  375.3 50.2 %all-to-all-start = ((f32[1,1,256,1024]{3,1,0,2:T(1,128)}), f32[1,1,256,1024]{3,1,0,2:T(1,128)}, u32[]{:S(2)}, u32[]{:S(2)}) async-start(f32[1,1,256,1024]{3,1,0,2:T(1,128)} %copy.74), calls=%async_computation | async-start | bytes 2097152 | tf_op jit(solution)/shard_map/all_to_all | solution.py:105
  380.8 154.3 %all-gather.8.cloned.1.call-start = ((), (), s32[]{:S(2)}) async-start(), calls=%async_computation.10 | async-start | bytes 2129920 | tf_op jit(solution)/shard_map/all_gather | solution.py:74
  396.1 139.0 %copy-start.4 = (bf16[1,256,1024]{2,1,0:T(8,128)(2,1)S(1)}, bf16[1,256,1024]{2,1,0:T(8,128)(2,1)}, u32[]{:S(2)}) copy-start(bf16[1,256,1024]{2,1,0:T(8,128)(2,1)} %param.16) | copy-start | bytes 1572868
  425.5 112.2 %copy-start.5 = (f32[1024]{0:T(1024)S(1)}, f32[1024]{0:T(1024)}, u32[]{:S(2)}) copy-start(f32[1024]{0:T(1024)} %param.24) | copy-start | bytes 12292
  428.6 120.4 %copy-start.7 = (bf16[128,64]{0,1:T(8,128)(2,1)S(1)}, bf16[128,64]{0,1:T(8,128)(2,1)}, u32[]{:S(2)}) copy-start(bf16[128,64]{0,1:T(8,128)(2,1)} %param.25) | copy-start | bytes 49156
  428.6 132.0 %copy-start.8 = (bf16[64,128]{1,0:T(8,128)(2,1)S(1)}, bf16[64,128]{1,0:T(8,128)(2,1)}, u32[]{:S(2)}) copy-start(bf16[64,128]{1,0:T(8,128)(2,1)} %param.26) | copy-start | bytes 49156
  538.7 33.6 %all-to-all-start.3 = ((bf16[64,1,4,1024]{3,2,1,0:T(4,128)(2,1)}), bf16[64,1,4,1024]{3,2,1,0:T(4,128)(2,1)S(1)}, u32[]{:S(2)}, u32[]{:S(2)}) async-start(bf16[64,1,4,1024]{3,2,1,0:T(4,128)(2,1)} %stack.6), calls=%async_computation.3 | async-start | bytes 1048576 | tf_op jit(solution)/shard_map/all_to_all | solution.py:134
  548.9 301.0 %all-reduce.5.cloned.1.call-start = ((), (), s32[]{:S(2)}) async-start(), calls=%async_computation.11 | async-start | bytes 2097152
  571.6 6.5 copy-start.11
  571.6 280.4 %copy-start.9 = (f32[1024]{0:T(1024)S(1)}, f32[1024]{0:T(1024)}, u32[]{:S(2)}) copy-start(f32[1024]{0:T(1024)} %param.27) | copy-start | bytes 12292
  849.9 101.9 %copy-start.12 = (bf16[1024,1024]{0,1:T(8,128)(2,1)S(1)}, bf16[1024,1024]{0,1:T(8,128)(2,1)}, u32[]{:S(2)}) copy-start(bf16[1024,1024]{0,1:T(8,128)(2,1)} %all-gather.6.cloned.1.call-done) | copy-start | bytes 6291460
  972.3 26.8 %all-to-all-start.5 = ((f32[1,1,256,16]{3,1,0,2:T(1,128)}), f32[1,1,256,16]{3,1,0,2:T(1,128)S(1)}, u32[]{:S(2)}, u32[]{:S(2)}) async-start(f32[1,1,256,16]{3,1,0,2:T(1,128)} %bitcast.69), calls=%async_computation.5 | async-start | bytes 262144 | tf_op jit(solution)/shard_map/all_to_all | solution.py:103
  999.1 23.8 %all-to-all-start.6 = ((f32[1,1,256,16]{3,1,0,2:T(1,128)}), f32[1,1,256,16]{3,1,0,2:T(1,128)S(1)}, u32[]{:S(2)}, u32[]{:S(2)}) async-start(f32[1,1,256,16]{3,1,0,2:T(1,128)} %bitcast.71), calls=%async_computation.6 | async-start | bytes 262144 | tf_op jit(solution)/shard_map/all_to_all | solution.py:104
  1022.9 51.3 %all-to-all-start.4 = ((f32[1,1,256,1024]{3,1,0,2:T(1,128)}), f32[1,1,256,1024]{3,1,0,2:T(1,128)}, u32[]{:S(2)}, u32[]{:S(2)}) async-start(f32[1,1,256,1024]{3,1,0,2:T(1,128)} %copy.84), calls=%async_computation.4 | async-start | bytes 2097152 | tf_op jit(solution)/shard_map/all_to_all | solution.py:105
  1028.9 346.1 %all-reduce.7.cloned.1.call-start = ((), (), s32[]{:S(2)}) async-start(), calls=%async_computation.12 | async-start | bytes 2097152
  1031.5 45.8 %copy-start = (bf16[1024,1024]{0,1:T(8,128)(2,1)S(1)}, bf16[1024,1024]{0,1:T(8,128)(2,1)}, u32[]{:S(2)}) copy-start(bf16[1024,1024]{0,1:T(8,128)(2,1)} %all-gather.8.cloned.1.call-done) | copy-start | bytes 6291460
  1108.0 367.9 %copy-start.2 = (bf16[1,256,1024]{2,1,0:T(8,128)(2,1)S(1)}, bf16[1,256,1024]{2,1,0:T(8,128)(2,1)}, u32[]{:S(2)}) copy-start(bf16[1,256,1024]{2,1,0:T(8,128)(2,1)} %copy-done.1) | copy-start | bytes 1572868
  (1 other events, 1.0 us)
Sparse Core Ops, SparseCore 0:
  22.9 141.5 all-gather.5
  167.5 142.5 all-gather.3
  393.9 141.1 all-gather.7
  576.3 273.5 all-reduce.4
  1110.2 264.7 all-reduce.6
